TPU v7x, 128 devices: a whole 4x4x4 slice. The times are simulated.
128 devices in a mesh: req: 32 (over z, x, core), mlp: 4 (over y).
Axes of the slice: x: 4, y: 4, z: 4, core: 2. Of those that a mesh axis runs over, the one named last changes fastest.
Arguments:
- residual_in: bfloat16 [32768, 1664], P('req'), may hold values from -6 to 6
- lengths: int32 [4096], P(('req', 'mlp')), may hold values from 0 to 16, as said below
- owners: int32 [4096], P(('req', 'mlp')), may hold values from 0 to 31, as said below
- merge_dest: int32 [32768], P('req'), may hold values from 0 to 255, as said below
- segment_ids: int32 [32768], P('req'), may hold values from 0 to 3, as said below
- norm2_gain: float32 [1664], replicated, may hold values from 0.5 to 1.5
- norm2_bias: float32 [1664], replicated, may hold values from -3 to 3
- up_weight: bfloat16 [4096, 1664], P('mlp'), may hold values from -0.15625 to 0.15625
- up_bias: float32 [4096], P('mlp'), may hold values from -3 to 3
- down_weight: bfloat16 [4096, 1664], P('mlp'), may hold values from -0.09375 to 0.09375
- down_bias: float32 [1664], replicated, may hold values from -3 to 3
- proj_weight: bfloat16 [6656, 1664], P('mlp'), may hold values from -0.078125 to 0.078125
- norm3_gain: float32 [1664], replicated, may hold values from 0.5 to 1.5
- norm3_bias: float32 [1664], replicated, may hold values from -3 to 3
- next_weight: bfloat16 [1664, 3, 1664], P('req'), may hold values from -0.15625 to 0.15625
Outputs:
- merged_out: bfloat16 [16384, 1664], P(('req', 'mlp'))
- next_mixed: bfloat16 [16384, 1664], P(('req', 'mlp'))
Inputs may be any that keep to these rules, and one draw needn't show every extreme that they name: The 32 pieces of each block of 256 tokens (one device, req-major order) have lengths that are multiples of 4 and sum to 256; in every block one piece has exactly 16 tokens. The owners of the 32 pieces of one block are a permutation of 0 to 31; for each index of mlp, one piece of 16 tokens of each block of that index goes to one owner shared by all blocks of that index. `merge_dest`: within each device block a permutation of 0 to 255 that maps the tokens of each piece onto that piece's own positions. `segment_ids`: the four tokens of a block whose merge_dest values have the same quotient by 4 carry one segment id.
All inputs are finite; a program needn't handle non-finite values.
Results may differ from a plain program's by a relative error of at most 0.023.
Values may be sent and summed in bfloat16 or wider, within the bound.
No kernel may reach another device: no remote copies, remote signals or barrier semaphores. Data moves between devices by JAX's collectives and lax.ppermute only.
A program may use at most 128 MiB of HBM per device.

v0:
```python
import math
import jax
import jax.numpy as jnp
from jax import lax
from jax.sharding import PartitionSpec as P

HEAD_DIM = 104
EPSILON = 1e-06


def layer_norm(rows, gain, bias):
    values = rows.astype(jnp.float32)
    mean_value = jnp.mean(values, axis=-1, keepdims=True)
    centred = values - mean_value
    spread = jnp.mean(centred * centred, axis=-1, keepdims=True)
    return centred * lax.rsqrt(spread + EPSILON) * gain + bias


def block_attention(heads_in, slot_tags):
    queries = heads_in[:, :, 0]
    key_rows = heads_in[:, :, 1]
    value_rows = heads_in[:, :, 2]
    score_scale = 1.0 / math.sqrt(heads_in.shape[-1])
    scores = (
        jnp.einsum("bqhe,bkhe->bhqk", queries, key_rows, preferred_element_type=jnp.float32)
        * score_scale
    )
    slot_total = heads_in.shape[1]
    itself = lax.broadcasted_iota(jnp.int32, (slot_total, slot_total), 0) == lax.broadcasted_iota(
        jnp.int32, (slot_total, slot_total), 1
    )
    live_slots = slot_tags >= 0
    same_request = slot_tags[:, :, None] == slot_tags[:, None, :]
    allowed = same_request & live_slots[:, None, :] | itself[None]
    weights = jnp.where(allowed[:, None], jnp.exp(scores), 0.0)
    probs = (weights / jnp.sum(weights, axis=-1, keepdims=True)).astype(jnp.bfloat16)
    mixed_out = jnp.einsum("bhqk,bkhe->bqhe", probs, value_rows, preferred_element_type=jnp.float32)
    mixed_out = jnp.where(live_slots[:, :, None, None], mixed_out, 0.0)
    return mixed_out.astype(jnp.bfloat16)


def body(
    residual_in,
    lengths,
    owners,
    merge_dest,
    segment_ids,
    norm2_gain,
    norm2_bias,
    up_weight,
    up_bias,
    down_weight,
    down_bias,
    proj_weight,
    norm3_gain,
    norm3_bias,
    next_weight,
):
    group_rows, model_width = residual_in.shape
    lane_count = lax.axis_size("mlp")
    sender_count = lax.axis_size("req")
    lane_index = lax.axis_index("mlp")
    own_rows = group_rows // lane_count
    merged_rows = own_rows // 4
    slot_count = 2 * merged_rows // sender_count
    normed = layer_norm(residual_in, norm2_gain, norm2_bias).astype(jnp.bfloat16)
    upward = lax.dot_general(
        normed, up_weight, (((1,), (1,)), ((), ())), preferred_element_type=jnp.float32
    )
    hidden = jax.nn.gelu(upward + up_bias, approximate=False).astype(jnp.bfloat16)
    partial_sums = jnp.dot(hidden, down_weight, preferred_element_type=jnp.float32)
    places = merge_dest.reshape(lane_count, own_rows)
    block_ids = lax.broadcasted_iota(jnp.int32, (lane_count, own_rows), 0)
    token_ids = lax.broadcasted_iota(jnp.int32, (lane_count, own_rows), 1)
    sources = jnp.zeros((lane_count, own_rows), jnp.int32).at[block_ids, places].set(token_ids)
    block_offset = own_rows * lax.broadcasted_iota(jnp.int32, (lane_count, merged_rows, 4), 0)
    group_index = sources.reshape(lane_count, merged_rows, 4) + block_offset
    quadrant_rows = lax.dynamic_index_in_dim(group_index, lane_index, 2, False).reshape(-1)
    feed_out = lax.psum(partial_sums.astype(jnp.bfloat16), "mlp").astype(jnp.float32)
    layer_out = (residual_in.astype(jnp.float32) + feed_out + down_bias).astype(jnp.bfloat16)
    quarter = jnp.take(layer_out, quadrant_rows, axis=0)
    projected = lax.psum_scatter(
        jnp.dot(quarter, proj_weight, preferred_element_type=jnp.float32).astype(jnp.bfloat16),
        "mlp",
        scatter_dimension=0,
        tiled=True,
    )
    first_tokens = lax.dynamic_index_in_dim(group_index[:, :, 0], lane_index, 0, False)
    row_segment = jnp.take(segment_ids, first_tokens, axis=0)
    counts = lengths // 4
    starts = jnp.cumsum(counts) - counts
    index = lax.broadcasted_iota(jnp.int32, (merged_rows, 1), 0)
    inside = ((index >= starts[None, :]) & (index < (starts + counts)[None, :])).astype(jnp.int32)
    owner_of = jnp.sum(inside * owners[None, :], axis=1)
    rank = index[:, 0] - jnp.sum(inside * starts[None, :], axis=1)
    target = owner_of * slot_count + rank
    slot_ids = lax.broadcasted_iota(jnp.int32, (sender_count * slot_count, 1), 0)
    route_hits = slot_ids == target[None, :]
    outgoing = jnp.dot(
        route_hits.astype(jnp.bfloat16), projected, preferred_element_type=jnp.float32
    ).astype(jnp.bfloat16)
    sent_tags = jnp.sum(route_hits.astype(jnp.int32) * (row_segment + 1)[None, :], axis=1) - 1
    received, arrived_tags = (
        lax.all_to_all(outgoing, "req", split_axis=0, concat_axis=0, tiled=True),
        lax.all_to_all(sent_tags, "req", split_axis=0, concat_axis=0, tiled=True),
    )
    normed3 = layer_norm(received, norm3_gain, norm3_bias).astype(jnp.bfloat16)
    recv_rows = received.shape[0]
    piece = lax.all_gather(next_weight, "req", axis=0, tiled=True)
    heads_in = jnp.dot(
        normed3, piece.reshape(piece.shape[0], -1), preferred_element_type=jnp.float32
    )
    heads_in = heads_in.astype(jnp.bfloat16).reshape(1, recv_rows, 3, -1, HEAD_DIM)
    next_mixed = block_attention(heads_in, arrived_tags.reshape(1, recv_rows)).reshape(
        recv_rows, model_width
    )
    return (received, next_mixed)


def solution(mesh):
    return jax.shard_map(
        body,
        mesh=mesh,
        in_specs=(
            P("req", None),
            P(("req", "mlp")),
            P(("req", "mlp")),
            P("req"),
            P("req"),
            P(),
            P(),
            P("mlp", None),
            P("mlp"),
            P("mlp", None),
            P(),
            P("mlp", None),
            P(),
            P(),
            P("req", None, None),
        ),
        out_specs=(P(("req", "mlp"), None), P(("req", "mlp"), None)),
        check_vma=False,
    )
```

profile of v0, /device:TPU:1, one launch (start us, length us, event | category | flops | bytes accessed | tf_op | source)
XLA Modules:
  0.0 286.2 jit_solution(13230346240546526583)
XLA Ops:
  8.0 0.0 copy-start
  8.0 0.0 all-reduce.2.cloned.1.call-start
  8.1 0.0 copy-start.3
  8.1 2.6 convert_reduce_fusion
  10.8 0.5 copy-done.3
  11.2 1.0 fusion.2
  12.3 0.0 copy-start.9
  12.3 0.0 copy-start.12
  12.3 0.0 copy-start.11
  12.3 20.5 %convolution_convert_fusion.1 = bf16[1024,1664]{1,0:T(8,128)(2,1)} fusion(bf16[1024,1664]{1,0:T(8,128)(2,1)S(1)} %copy-done, bf16[1024,1664]{1,0:T(8,128)(2,1)} %param.22, bf16[1024,1664]{1,0:T(8,128)(2,1)} %param.15, f32[1664]{0:T(1024)S(1)} %copy-done.13, f32[1664]{0:T(1024)S(1)} %copy-done.14, f32[1024]{0:T(1024)S(1)} %add_rsqrt_fusion.1, ...), kind=kOutput, calls=%fused_computation.34 | convolution fusion | flops 7060455424 | bytes 13657088 | tf_op jit(solution)/shard_map/dot_general | solution.py:71
  32.9 0.0 all-reduce.2.cloned.1.call-update
  32.9 0.0 reduce-scatter.2.cloned.1.call-start
  33.0 0.1 multiply_reduce_fusion
  33.1 0.1 and_reduce_fusion
  33.2 4.5 %scatter_custom_fusion = s32[1024]{0:T(1024)S(1)} fusion(s32[1024]{0:T(1024)S(1)} %bitcast.53, s32[1024]{0:T(1024)S(1)} %bitcast.54, s32[]{:T(128)} %constant.46.clone.1), kind=kCustom, calls=%fused_computation.124 | custom fusion | bytes 4100
  37.7 0.1 reshape.396
  37.8 0.1 broadcast_add_fusion
  37.9 0.2 fusion.116
  38.2 0.1 reshape.398
  38.2 0.7 reshape.397
  38.9 0.7 compare_and_fusion
  39.6 76.7 %all-reduce.2.cloned.1.call-done = bf16[1024,1664]{1,0:T(8,128)(2,1)} async-done(((bf16[1024,1664]{1,0:T(8,128)(2,1)}), bf16[1024,1664]{1,0:T(8,128)(2,1)}) %all-reduce.2.cloned.1.call-update) | async-done | bytes 3407888 | tf_op jit(solution)/shard_map/psum | solution.py:79
  116.3 0.0 copy-done.4
  116.3 4.8 %fusion.7 = bf16[1024,1664]{1,0:T(8,128)(2,1)} fusion(bf16[1024,1664]{1,0:T(8,128)(2,1)S(1)} %copy-done.4, bf16[1024,1664]{1,0:T(8,128)(2,1)} %all-reduce.2.cloned.1.call-done, f32[1664]{0:T(1024)S(1)} %copy-done.8), kind=kLoop, calls=%fused_computation.13 | loop fusion | flops 8519680 | bytes 10230272 | tf_op jit(solution)/shard_map/convert_element_type | solution.py:80
  121.1 4.5 %gather_fusion = bf16[256,1664]{1,0:T(8,128)(2,1)S(1)} fusion(bf16[1024,1664]{1,0:T(8,128)(2,1)} %fusion.7, s32[1024]{0:T(1024)S(1)} %pad_clamp_fusion.1), kind=kCustom, calls=%fused_computation | custom fusion | bytes 1704960 | tf_op jit(solution)/shard_map/jit(_take)/gather | solution.py:81
  125.6 0.0 copy-start.5
  125.6 0.0 copy-start.16
  125.7 0.0 copy-start.2
  125.7 0.0 copy-start.10
  125.7 5.5 %convolution_convert_fusion.2 = bf16[256,1664]{1,0:T(8,128)(2,1)} fusion(bf16[1664,1664]{1,0:T(8,128)(2,1)} %param.26, bf16[256,1664]{1,0:T(8,128)(2,1)S(1)} %gather_fusion, pred[256]{0:T(512)(128)(4,1)S(1)} %compare_and_fusion), kind=kOutput, calls=%fused_computation.40 | convolution fusion | flops 1418526720 | bytes 7241984 | tf_op jit(solution)/shard_map/dot_general | solution.py:83
  131.2 0.0 reduce-scatter.2.cloned.1.call-update
  131.2 0.0 all-gather.2.cloned.1.call-start
  131.2 1.1 copy.42
  132.4 0.0 all-gather.2.cloned.1.call-update
  132.4 0.1 copy.40
  132.5 0.1 reduce-window.8
  132.6 0.1 reduce.6
  132.7 0.1 dynamic-slice_reduce_fusion.1
  132.8 0.7 gather_fusion.1
  133.6 0.1 select_reduce_fusion.2
  133.7 0.1 select_reduce_fusion
  133.8 0.1 sub.46
  133.9 14.4 %all_to_all.21 = s32[32,4,1]{1,2,0:T(1,128)S(1)} all-to-all(s32[32,4,1]{1,2,0:T(1,128)S(1)} %bitcast.51), channel_id=1, replica_groups=mesh['req'=32,'mlp'=4] {'req'}, dimensions={0} | all-to-all | bytes 1024 | tf_op jit(solution)/shard_map/all_to_all | solution.py:105
  148.3 0.5 broadcast.328
  148.8 0.7 reduce.18
  149.5 0.1 all_to_all.18
  149.6 3.1 %reduce-scatter.2.cloned.1.call-done = bf16[64,1664]{1,0:T(8,128)(2,1)} async-done(((bf16[256,1664]{1,0:T(8,128)(2,1)}), bf16[64,1664]{1,0:T(8,128)(2,1)}) %reduce-scatter.2.cloned.1.call-update) | async-done | bytes 213008 | tf_op jit(solution)/shard_map/reduce_scatter | solution.py:82
  152.7 1.3 convolution_convert_fusion.3
  154.0 0.9 all_to_all.14
  154.9 8.8 %all-to-all-start = ((bf16[32,4,1664]{2,1,0:T(4,128)(2,1)}), bf16[32,4,1664]{2,1,0:T(4,128)(2,1)S(1)}, u32[]{:S(2)}, u32[]{:S(2)}) async-start(bf16[32,4,1664]{2,1,0:T(4,128)(2,1)} %all_to_all.14), calls=%async_computation.1 | async-start | bytes 851968 | tf_op jit(solution)/shard_map/all_to_all | solution.py:104
  163.7 0.1 fusion.74
  163.9 10.4 %all-to-all-done = bf16[32,4,1664]{2,1,0:T(4,128)(2,1)S(1)} async-done(((bf16[32,4,1664]{2,1,0:T(4,128)(2,1)}), bf16[32,4,1664]{2,1,0:T(4,128)(2,1)S(1)}, u32[]{:S(2)}, u32[]{:S(2)}) %all-to-all-start) | async-done | bytes 426016 | tf_op jit(solution)/shard_map/all_to_all | solution.py:104
  174.3 0.2 convert_reduce_fusion.1
  174.5 0.4 fusion.65
  175.0 0.4 fusion.68
  175.4 0.1 convert_element_type.63
  175.5 0.9 all_to_all.16
  176.4 44.4 %all-gather.2.cloned.1.call-done = bf16[1664,3,1664]{2,1,0:T(4,128)(2,1)} async-done(((bf16[52,3,1664]{2,1,0:T(4,128)(2,1)}), bf16[1664,3,1664]{2,1,0:T(4,128)(2,1)}) %all-gather.2.cloned.1.call-update) | async-done | bytes 16613392 | tf_op jit(solution)/shard_map/all_gather | solution.py:109
  220.8 36.4 %copy.43 = bf16[1664,3,1664]{0,2,1:T(8,128)(2,1)} copy(bf16[1664,3,1664]{2,1,0:T(4,128)(2,1)} %all-gather.2.cloned.1.call-done) | data formatting | bytes 33226752 | tf_op jit(solution)/shard_map/all_gather | solution.py:109
  257.2 11.7 %convolution_convert_fusion = bf16[128,4992]{1,0:T(8,128)(2,1)} fusion(bf16[128,1664]{1,0:T(8,128)(2,1)S(1)} %convert_element_type.63, bf16[1664,4992]{0,1:T(8,128)(2,1)} %bitcast.47), kind=kOutput, calls=%fused_computation.15 | convolution fusion | flops 2127151104 | bytes 18317312 | tf_op jit(solution)/shard_map/dot_general | solution.py:110
  268.8 2.6 copy.44
  271.4 2.5 fusion.60
  273.9 2.8 fusion.62
  276.8 2.0 copy.46
  (45 shorter events, 0.2 us)
Async XLA Ops:
  8.0 4.3 %copy-start = (bf16[1024,1664]{1,0:T(8,128)(2,1)S(1)}, bf16[1024,1664]{1,0:T(8,128)(2,1)}, u32[]{:S(2)}) copy-start(bf16[1024,1664]{1,0:T(8,128)(2,1)} %param.24) | copy-start | bytes 10223620
  8.0 4.3 %copy-start.15 = (f32[1024]{0:T(1024)S(1)}, f32[1024]{0:T(1024)}, u32[]{:S(2)}) copy-start(f32[1024]{0:T(1024)} %param.23) | copy-start | bytes 12292
  8.0 4.3 %copy-start.13 = (f32[1664]{0:T(1024)S(1)}, f32[1664]{0:T(1024)}, u32[]{:S(2)}) copy-start(f32[1664]{0:T(1024)} %param.21) | copy-start | bytes 19972
  8.0 108.3 %all-reduce.2.cloned.1.call-start = ((), (), s32[]{:S(2)}) async-start(), calls=%async_computation.3 | async-start | bytes 6815744 | tf_op jit(solution)/shard_map/psum | solution.py:79
  8.1 3.1 %copy-start.3 = (bf16[1024,1664]{1,0:T(8,128)(2,1)S(1)}, bf16[1024,1664]{1,0:T(8,128)(2,1)}, u32[]{:S(2)}) copy-start(bf16[1024,1664]{1,0:T(8,128)(2,1)} %param.15) | copy-start | bytes 10223620
  8.1 4.2 %copy-start.14 = (f32[1664]{0:T(1024)S(1)}, f32[1664]{0:T(1024)}, u32[]{:S(2)}) copy-start(f32[1664]{0:T(1024)} %param.20) | copy-start | bytes 19972
  12.3 20.6 %copy-start.9 = (s32[1024]{0:T(1024)S(1)}, s32[1024]{0:T(1024)}, u32[]{:S(2)}) copy-start(s32[1024]{0:T(1024)} %param.18) | copy-start | bytes 12292
  12.3 20.7 %copy-start.12 = (s32[2]{0:T(128)S(1)}, s32[2]{0:T(128)}, u32[]{:S(2)}) copy-start(s32[2]{0:T(128)} %constant.153) | copy-start | bytes 28
  12.3 20.7 %copy-start.11 = (s32[2]{0:T(128)S(1)}, s32[2]{0:T(128)}, u32[]{:S(2)}) copy-start(s32[2]{0:T(128)} %constant.156) | copy-start | bytes 28
  32.9 83.4 %copy-start.4 = (bf16[1024,1664]{1,0:T(8,128)(2,1)S(1)}, bf16[1024,1664]{1,0:T(8,128)(2,1)}, u32[]{:S(2)}) copy-start(bf16[1024,1664]{1,0:T(8,128)(2,1)} %param.15) | copy-start | bytes 10223620
  32.9 83.4 %copy-start.8 = (f32[1664]{0:T(1024)S(1)}, f32[1664]{0:T(1024)}, u32[]{:S(2)}) copy-start(f32[1664]{0:T(1024)} %param.25) | copy-start | bytes 19972
  32.9 119.8 %reduce-scatter.2.cloned.1.call-start = ((), (), s32[]{:S(2)}) async-start(), calls=%async_computation.4 | async-start | bytes 1064960 | tf_op jit(solution)/shard_map/reduce_scatter | solution.py:82
  125.6 5.6 %copy-start.5 = (bf16[52,3,1664]{2,0,1:T(8,128)(2,1)S(1)}, bf16[52,3,1664]{2,0,1:T(8,128)(2,1)}, u32[]{:S(2)}) copy-start(bf16[52,3,1664]{2,0,1:T(8,128)(2,1)} %param.29) | copy-start | bytes 1557508
  125.6 6.8 %copy-start.16 = (s32[32]{0:T(128)S(1)}, s32[32]{0:T(128)}, u32[]{:S(2)}) copy-start(s32[32]{0:T(128)} %param.16) | copy-start | bytes 388
  125.7 7.2 %copy-start.2 = (s32[1024]{0:T(1024)S(1)}, s32[1024]{0:T(1024)}, u32[]{:S(2)}) copy-start(s32[1024]{0:T(1024)} %param.19) | copy-start | bytes 12292
  125.7 7.9 %copy-start.10 = (s32[32]{0:T(128)S(1)}, s32[32]{0:T(128)}, u32[]{:S(2)}) copy-start(s32[32]{0:T(128)} %param.17) | copy-start | bytes 388
  131.2 43.8 %copy-start.6 = (f32[1664]{0:T(1024)S(1)}, f32[1664]{0:T(1024)}, u32[]{:S(2)}) copy-start(f32[1664]{0:T(1024)} %param.28) | copy-start | bytes 19972
  131.2 43.8 %copy-start.7 = (f32[1664]{0:T(1024)S(1)}, f32[1664]{0:T(1024)}, u32[]{:S(2)}) copy-start(f32[1664]{0:T(1024)} %param.27) | copy-start | bytes 19972
  131.2 89.6 %all-gather.2.cloned.1.call-start = ((), (), s32[]{:S(2)}) async-start(), calls=%async_computation.5 | async-start | bytes 22843392 | tf_op jit(solution)/shard_map/all_gather | solution.py:109
  154.9 19.4 %all-to-all-start = ((bf16[32,4,1664]{2,1,0:T(4,128)(2,1)}), bf16[32,4,1664]{2,1,0:T(4,128)(2,1)S(1)}, u32[]{:S(2)}, u32[]{:S(2)}) async-start(bf16[32,4,1664]{2,1,0:T(4,128)(2,1)} %all_to_all.14), calls=%async_computation.1 | async-start | bytes 851968 | tf_op jit(solution)/shard_map/all_to_all | solution.py:104
  268.8 9.9 %copy-start.1 = (bf16[1024,1664]{1,0:T(8,128)(2,1)S(1)}, bf16[1024,1664]{1,0:T(8,128)(2,1)}, u32[]{:S(2)}) copy-start(bf16[1024,1664]{1,0:T(8,128)(2,1)} %param.24) | copy-start | bytes 10223620
Sparse Core Ops, SparseCore 0:
  33.0 83.2 all-reduce.1
  131.3 21.3 reduce-scatter.1
Sparse Core Ops, SparseCore 1:
  134.3 86.4 all-gather.1
where the time goes:
time: 288 us; the launch traced here: 286 us
  waiting for transfers between devices  135 us (47%)
  local copies, waits for them, and re-layouts  56.2 us (20%)
  matrix products  44.3 us (15%)
  between operations  15.9 us (6%)
  blocking collectives  14.4 us (5%)
  other arithmetic  11.7 us (4%)
  starting transfers between devices  8.95 us (3%)
    psum x1, waiting for transfers between devices, body(): lax.psum(partial_sums.astype(jnp.bfloat16), 'mlp').astype(jnp.float32)  76.7 us
    all_gather x1, waiting for transfers between devices, body(): piece = lax.all_gather(next_weight, 'req', axis=0, tiled=True)  44.4 us
    all_gather x1, local copies, waits for them, and re-layouts, body(): piece = lax.all_gather(next_weight, 'req', axis=0, tiled=True)  36.4 us
    dot_general x1, matrix products, body(): jnp.dot(hidden, down_weight, preferred_element_type=jnp.float32)  20.5 us
    all_to_all x1, blocking collectives, body(): lax.all_to_all(sent_tags, 'req', split_axis=0, concat_axis=0, tiled=True)  14.4 us
    dot_general x1, matrix products, body(): jnp.dot(normed3, piece.reshape(piece.shape[0], -1), preferred_element_typ...  11.7 us
    all_to_all x1, waiting for transfers between devices, body(): lax.all_to_all(outgoing, 'req', split_axis=0, concat_axis=0, tiled=True)  10.4 us
    all_to_all x1, starting transfers between devices, body(): lax.all_to_all(outgoing, 'req', split_axis=0, concat_axis=0, tiled=True)  8.83 us
  transfers between devices with their start and end apart: 4, of which 4 were waited for; matrix products, arithmetic and copies ran while one was open for 5% of the time, Pallas kernels for 0%

commit v1 on v0

--- a/solution.py
+++ b/solution.py
@@ -6,6 +6,12 @@
 
 HEAD_DIM = 104
 EPSILON = 1e-06
+
+
+def gather_and_add(x, mesh_axis):
+    parts = lax.all_gather(x, mesh_axis, axis=0, tiled=False)
+    total = parts.sum(axis=0)
+    return total
 
 
 def layer_norm(rows, gain, bias):
@@ -76,7 +82,7 @@
     block_offset = own_rows * lax.broadcasted_iota(jnp.int32, (lane_count, merged_rows, 4), 0)
     group_index = sources.reshape(lane_count, merged_rows, 4) + block_offset
     quadrant_rows = lax.dynamic_index_in_dim(group_index, lane_index, 2, False).reshape(-1)
-    feed_out = lax.psum(partial_sums.astype(jnp.bfloat16), "mlp").astype(jnp.float32)
+    feed_out = gather_and_add(partial_sums.astype(jnp.bfloat16), "mlp").astype(jnp.float32)
     layer_out = (residual_in.astype(jnp.float32) + feed_out + down_bias).astype(jnp.bfloat16)
     quarter = jnp.take(layer_out, quadrant_rows, axis=0)
     projected = lax.psum_scatter(

time: 288 us -> 346 us (1.20)
  waiting for transfers between devices: 135 us -> 184 us
  other arithmetic: 11.7 us -> 20.7 us
    all_gather x0 -> x1, waiting for transfers between devices: none -> 125 us  [gather_and_add(): parts = lax.all_gather(x, mesh_axis, axis=0, tiled=False)]
    psum x1 -> x0, waiting for transfers between devices: 76.7 us -> none  [body(): lax.psum(partial_sums.astype(jnp.bfloat16), 'mlp').astype(jnp.float32)]
    reduce_sum x0 -> x1, other arithmetic: none -> 9.72 us  [gather_and_add(): total = parts.sum(axis=0)]
  transfers between devices with their start and end apart: 4 -> 4, of which waited for: 4 -> 4; matrix products, arithmetic and copies ran while one was open for 5% -> 3% of each run, Pallas kernels for 0% -> 0%
where the time goes in v1:
time: 346 us; the launch traced here: 344 us
  waiting for transfers between devices  184 us (53%)
  local copies, waits for them, and re-layouts  55.7 us (16%)
  matrix products  44.3 us (13%)
  other arithmetic  20.7 us (6%)
  between operations  15.9 us (5%)
  blocking collectives  14.4 us (4%)
  starting transfers between devices  8.96 us (3%)
    all_gather x1, waiting for transfers between devices, gather_and_add(): parts = lax.all_gather(x, mesh_axis, axis=0, tiled=False)  125 us
    all_gather x1, waiting for transfers between devices, body(): piece = lax.all_gather(next_weight, 'req', axis=0, tiled=True)  44.4 us
    all_gather x1, local copies, waits for them, and re-layouts, body(): piece = lax.all_gather(next_weight, 'req', axis=0, tiled=True)  36.4 us
    dot_general x1, matrix products, body(): jnp.dot(hidden, down_weight, preferred_element_type=jnp.float32)  20.4 us
    all_to_all x1, blocking collectives, body(): lax.all_to_all(sent_tags, 'req', split_axis=0, concat_axis=0, tiled=True)  14.4 us
    dot_general x1, matrix products, body(): jnp.dot(normed3, piece.reshape(piece.shape[0], -1), preferred_element_typ...  11.7 us
    all_to_all x1, waiting for transfers between devices, body(): lax.all_to_all(outgoing, 'req', split_axis=0, concat_axis=0, tiled=True)  10.4 us
    reduce_sum x1, other arithmetic, gather_and_add(): total = parts.sum(axis=0)  9.72 us
  transfers between devices with their start and end apart: 4, of which 4 were waited for; matrix products, arithmetic and copies ran while one was open for 3% of the time, Pallas kernels for 0%

profile of v1, /device:TPU:1, one launch (start us, length us, event | category | flops | bytes accessed | tf_op | source)
XLA Modules:
  0.0 344.3 jit_solution(9405995481612286250)
XLA Ops:
  8.0 0.0 copy-start
  8.0 0.0 all-gather.6.cloned.1.call-start
  8.1 0.0 copy-start.3
  8.1 2.6 convert_reduce_fusion
  10.8 0.5 copy-done.3
  11.2 1.0 fusion.2
  12.3 0.0 copy-start.9
  12.3 0.0 copy-start.12
  12.3 0.0 copy-start.11
  12.3 20.4 %convolution_convert_fusion.1 = bf16[1024,1664]{1,0:T(8,128)(2,1)} fusion(bf16[1024,1664]{1,0:T(8,128)(2,1)S(1)} %copy-done, bf16[1024,1664]{1,0:T(8,128)(2,1)} %param.22, bf16[1024,1664]{1,0:T(8,128)(2,1)} %param.15, f32[1664]{0:T(1024)S(1)} %copy-done.13, f32[1664]{0:T(1024)S(1)} %copy-done.14, f32[1024]{0:T(1024)S(1)} %add_rsqrt_fusion.1, ...), kind=kOutput, calls=%fused_computation.34 | convolution fusion | flops 7060455424 | bytes 13657088 | tf_op jit(solution)/shard_map/dot_general | solution.py:77
  32.8 0.0 all-gather.6.cloned.1.call-update
  32.8 0.0 reduce-scatter.2.cloned.1.call-start
  32.9 0.1 multiply_reduce_fusion
  33.0 0.1 and_reduce_fusion
  33.1 4.5 %scatter_custom_fusion = s32[1024]{0:T(1024)S(1)} fusion(s32[1024]{0:T(1024)S(1)} %bitcast.55, s32[1024]{0:T(1024)S(1)} %bitcast.56, s32[]{:T(128)} %constant.47.clone.1), kind=kCustom, calls=%fused_computation.124 | custom fusion | bytes 4100
  37.6 0.1 reshape.396
  37.8 0.1 broadcast_add_fusion
  37.8 0.2 fusion.116
  38.1 0.1 reshape.398
  38.2 0.1 reshape.397
  38.3 125.4 %all-gather.6.cloned.1.call-done = bf16[4096,1664]{1,0:T(8,128)(2,1)} async-done(((bf16[1024,1664]{1,0:T(8,128)(2,1)}), bf16[4096,1664]{1,0:T(8,128)(2,1)}) %all-gather.6.cloned.1.call-update) | async-done | bytes 13631504 | tf_op jit(solution)/shard_map/all_gather | solution.py:12
  163.6 9.7 %reduce_sum.88 = bf16[1024,1664]{1,0:T(8,128)(2,1)} reduce(bf16[4,1024,1664]{2,1,0:T(8,128)(2,1)} %bitcast.49, bf16[]{:T(256)} %constant.148.clone.1), dimensions={0}, to_apply=%region_6.7 | reduce | flops 5111808 | bytes 17039362 | tf_op jit(solution)/shard_map/reduce_sum | solution.py:13
  173.4 0.0 copy-done.8
  173.4 4.7 %fusion.7 = bf16[1024,1664]{1,0:T(8,128)(2,1)} fusion(bf16[1024,1664]{1,0:T(8,128)(2,1)S(1)} %copy-done.4, bf16[1024,1664]{1,0:T(8,128)(2,1)} %reduce_sum.88, f32[1664]{0:T(1024)S(1)} %copy-done.8), kind=kLoop, calls=%fused_computation.13 | loop fusion | flops 8519680 | bytes 10230272 | tf_op jit(solution)/shard_map/convert_element_type | solution.py:86
  178.1 4.5 %gather_fusion = bf16[256,1664]{1,0:T(8,128)(2,1)S(1)} fusion(bf16[1024,1664]{1,0:T(8,128)(2,1)} %fusion.7, s32[1024]{0:T(1024)S(1)} %pad_clamp_fusion.1), kind=kCustom, calls=%fused_computation | custom fusion | bytes 1704960 | tf_op jit(solution)/shard_map/jit(_take)/gather | solution.py:87
  182.6 0.0 copy-start.5
  182.7 0.0 copy-start.16
  182.7 0.0 copy-start.2
  182.7 0.0 copy-start.10
  182.7 5.5 %convolution_convert_fusion.2 = bf16[256,1664]{1,0:T(8,128)(2,1)} fusion(bf16[1664,1664]{1,0:T(8,128)(2,1)} %param.26, bf16[256,1664]{1,0:T(8,128)(2,1)S(1)} %gather_fusion, pred[256]{0:T(512)(128)(4,1)S(1)} %compare_and_fusion), kind=kOutput, calls=%fused_computation.40 | convolution fusion | flops 1418526720 | bytes 7241984 | tf_op jit(solution)/shard_map/dot_general | solution.py:89
  188.2 0.0 reduce-scatter.2.cloned.1.call-update
  188.2 0.0 all-gather.4.cloned.1.call-start
  188.2 1.1 copy.42
  189.4 0.0 all-gather.4.cloned.1.call-update
  189.4 0.1 copy.40
  189.5 0.1 reduce-window.8
  189.6 0.1 reduce.7
  189.7 0.1 dynamic-slice_reduce_fusion.1
  189.8 0.7 gather_fusion.1
  190.6 0.1 select_reduce_fusion.2
  190.7 0.1 select_reduce_fusion
  190.8 0.1 sub.46
  190.9 14.4 %all_to_all.21 = s32[32,4,1]{1,2,0:T(1,128)S(1)} all-to-all(s32[32,4,1]{1,2,0:T(1,128)S(1)} %bitcast.53), channel_id=1, replica_groups=mesh['req'=32,'mlp'=4] {'req'}, dimensions={0} | all-to-all | bytes 1024 | tf_op jit(solution)/shard_map/all_to_all | solution.py:111
  205.3 0.5 broadcast.328
  205.8 0.7 reduce.19
  206.5 0.1 all_to_all.18
  206.6 4.2 %reduce-scatter.2.cloned.1.call-done = bf16[64,1664]{1,0:T(8,128)(2,1)} async-done(((bf16[256,1664]{1,0:T(8,128)(2,1)}), bf16[64,1664]{1,0:T(8,128)(2,1)}) %reduce-scatter.2.cloned.1.call-update) | async-done | bytes 213008 | tf_op jit(solution)/shard_map/reduce_scatter | solution.py:88
  210.9 1.3 convolution_convert_fusion.3
  212.2 0.9 all_to_all.14
  213.1 8.8 %all-to-all-start = ((bf16[32,4,1664]{2,1,0:T(4,128)(2,1)}), bf16[32,4,1664]{2,1,0:T(4,128)(2,1)S(1)}, u32[]{:S(2)}, u32[]{:S(2)}) async-start(bf16[32,4,1664]{2,1,0:T(4,128)(2,1)} %all_to_all.14), calls=%async_computation.1 | async-start | bytes 851968 | tf_op jit(solution)/shard_map/all_to_all | solution.py:110
  221.9 0.1 fusion.74
  222.0 10.4 %all-to-all-done = bf16[32,4,1664]{2,1,0:T(4,128)(2,1)S(1)} async-done(((bf16[32,4,1664]{2,1,0:T(4,128)(2,1)}), bf16[32,4,1664]{2,1,0:T(4,128)(2,1)S(1)}, u32[]{:S(2)}, u32[]{:S(2)}) %all-to-all-start) | async-done | bytes 426016 | tf_op jit(solution)/shard_map/all_to_all | solution.py:110
  232.4 0.2 convert_reduce_fusion.1
  232.7 0.4 fusion.65
  233.1 0.4 fusion.68
  233.5 0.1 convert_element_type.65
  233.7 0.9 all_to_all.16
  234.5 44.4 %all-gather.4.cloned.1.call-done = bf16[1664,3,1664]{2,1,0:T(4,128)(2,1)} async-done(((bf16[52,3,1664]{2,1,0:T(4,128)(2,1)}), bf16[1664,3,1664]{2,1,0:T(4,128)(2,1)}) %all-gather.4.cloned.1.call-update) | async-done | bytes 16613392 | tf_op jit(solution)/shard_map/all_gather | solution.py:115
  278.9 36.4 %copy.43 = bf16[1664,3,1664]{0,2,1:T(8,128)(2,1)} copy(bf16[1664,3,1664]{2,1,0:T(4,128)(2,1)} %all-gather.4.cloned.1.call-done) | data formatting | bytes 33226752 | tf_op jit(solution)/shard_map/all_gather | solution.py:115
  315.3 11.7 %convolution_convert_fusion = bf16[128,4992]{1,0:T(8,128)(2,1)} fusion(bf16[128,1664]{1,0:T(8,128)(2,1)S(1)} %convert_element_type.65, bf16[1664,4992]{0,1:T(8,128)(2,1)} %bitcast.48), kind=kOutput, calls=%fused_computation.15 | convolution fusion | flops 2127151104 | bytes 18317312 | tf_op jit(solution)/shard_map/dot_general | solution.py:116
  327.0 2.6 copy.44
  329.5 2.5 fusion.60
  332.1 2.8 fusion.62
  334.9 2.0 copy.46
  (46 shorter events, 0.2 us)
Async XLA Ops:
  8.0 4.3 %copy-start = (bf16[1024,1664]{1,0:T(8,128)(2,1)S(1)}, bf16[1024,1664]{1,0:T(8,128)(2,1)}, u32[]{:S(2)}) copy-start(bf16[1024,1664]{1,0:T(8,128)(2,1)} %param.24) | copy-start | bytes 10223620
  8.0 4.3 %copy-start.15 = (f32[1024]{0:T(1024)S(1)}, f32[1024]{0:T(1024)}, u32[]{:S(2)}) copy-start(f32[1024]{0:T(1024)} %param.23) | copy-start | bytes 12292
  8.0 4.3 %copy-start.13 = (f32[1664]{0:T(1024)S(1)}, f32[1664]{0:T(1024)}, u32[]{:S(2)}) copy-start(f32[1664]{0:T(1024)} %param.21) | copy-start | bytes 19972
  8.0 155.6 %all-gather.6.cloned.1.call-start = ((), (), s32[]{:S(2)}) async-start(), calls=%async_computation.5 | async-start | bytes 17039360 | tf_op jit(solution)/shard_map/all_gather | solution.py:12
  8.1 3.1 copy-start.3
  8.1 4.2 %copy-start.14 = (f32[1664]{0:T(1024)S(1)}, f32[1664]{0:T(1024)}, u32[]{:S(2)}) copy-start(f32[1664]{0:T(1024)} %param.20) | copy-start | bytes 19972
  12.3 20.6 %copy-start.9 = (s32[1024]{0:T(1024)S(1)}, s32[1024]{0:T(1024)}, u32[]{:S(2)}) copy-start(s32[1024]{0:T(1024)} %param.18) | copy-start | bytes 12292
  12.3 20.6 %copy-start.12 = (s32[2]{0:T(128)S(1)}, s32[2]{0:T(128)}, u32[]{:S(2)}) copy-start(s32[2]{0:T(128)} %constant.155) | copy-start | bytes 28
  12.3 20.7 %copy-start.11 = (s32[2]{0:T(128)S(1)}, s32[2]{0:T(128)}, u32[]{:S(2)}) copy-start(s32[2]{0:T(128)} %constant.158) | copy-start | bytes 28
  32.8 178.1 %reduce-scatter.2.cloned.1.call-start = ((), (), s32[]{:S(2)}) async-start(), calls=%async_computation.3 | async-start | bytes 1064960 | tf_op jit(solution)/shard_map/reduce_scatter | solution.py:88
  163.6 9.7 %copy-start.4 = (bf16[1024,1664]{1,0:T(8,128)(2,1)S(1)}, bf16[1024,1664]{1,0:T(8,128)(2,1)}, u32[]{:S(2)}) copy-start(bf16[1024,1664]{1,0:T(8,128)(2,1)} %param.15) | copy-start | bytes 10223620
  163.6 9.7 %copy-start.8 = (f32[1664]{0:T(1024)S(1)}, f32[1664]{0:T(1024)}, u32[]{:S(2)}) copy-start(f32[1664]{0:T(1024)} %param.25) | copy-start | bytes 19972
  182.6 5.6 %copy-start.5 = (bf16[52,3,1664]{2,0,1:T(8,128)(2,1)S(1)}, bf16[52,3,1664]{2,0,1:T(8,128)(2,1)}, u32[]{:S(2)}) copy-start(bf16[52,3,1664]{2,0,1:T(8,128)(2,1)} %param.29) | copy-start | bytes 1557508
  182.7 6.8 %copy-start.16 = (s32[32]{0:T(128)S(1)}, s32[32]{0:T(128)}, u32[]{:S(2)}) copy-start(s32[32]{0:T(128)} %param.16) | copy-start | bytes 388
  182.7 7.2 %copy-start.2 = (s32[1024]{0:T(1024)S(1)}, s32[1024]{0:T(1024)}, u32[]{:S(2)}) copy-start(s32[1024]{0:T(1024)} %param.19) | copy-start | bytes 12292
  182.7 7.9 %copy-start.10 = (s32[32]{0:T(128)S(1)}, s32[32]{0:T(128)}, u32[]{:S(2)}) copy-start(s32[32]{0:T(128)} %param.17) | copy-start | bytes 388
  188.2 44.9 %copy-start.6 = (f32[1664]{0:T(1024)S(1)}, f32[1664]{0:T(1024)}, u32[]{:S(2)}) copy-start(f32[1664]{0:T(1024)} %param.28) | copy-start | bytes 19972
  188.2 45.0 %copy-start.7 = (f32[1664]{0:T(1024)S(1)}, f32[1664]{0:T(1024)}, u32[]{:S(2)}) copy-start(f32[1664]{0:T(1024)} %param.27) | copy-start | bytes 19972
  188.2 90.7 %all-gather.4.cloned.1.call-start = ((), (), s32[]{:S(2)}) async-start(), calls=%async_computation.4 | async-start | bytes 22843392 | tf_op jit(solution)/shard_map/all_gather | solution.py:115
  213.1 19.4 %all-to-all-start = ((bf16[32,4,1664]{2,1,0:T(4,128)(2,1)}), bf16[32,4,1664]{2,1,0:T(4,128)(2,1)S(1)}, u32[]{:S(2)}, u32[]{:S(2)}) async-start(bf16[32,4,1664]{2,1,0:T(4,128)(2,1)} %all_to_all.14), calls=%async_computation.1 | async-start | bytes 851968 | tf_op jit(solution)/shard_map/all_to_all | solution.py:110
  327.0 9.9 %copy-start.1 = (bf16[1024,1664]{1,0:T(8,128)(2,1)S(1)}, bf16[1024,1664]{1,0:T(8,128)(2,1)}, u32[]{:S(2)}) copy-start(bf16[1024,1664]{1,0:T(8,128)(2,1)} %param.24) | copy-start | bytes 10223620
Sparse Core Ops, SparseCore 0:
  32.9 130.6 all-gather.5
  188.3 22.5 reduce-scatter.1
Sparse Core Ops, SparseCore 1:
  191.3 87.6 all-gather.3
